TPU v7x, 128 devices: a whole 4x4x4 slice. The times are simulated.
128 devices in a mesh: tile: 32 (over x, z, core), dp: 4 (over y).
Axes of the slice: x: 4, y: 4, z: 4, core: 2. Of those that a mesh axis runs over, the one named last changes fastest.
Arguments:
- fields: bfloat16 [4, 64, 64, 64, 128], P('dp', 'tile'), may hold values from -6 to 6
- cotangent: bfloat16 [4, 64, 64, 64, 128], P('dp', 'tile'), may hold values from -6 to 6
- is_ocean: int32 [64], P('tile'), may hold values from 0 to 1, as said below
- neighbours: int32 [64, 8], P('tile'), may hold values from -1 to 63, as said below
- kernel: float32 [7, 7, 128], replicated, may hold values from -0.875 to 0.875
- conv_bias: float32 [128], replicated, may hold values from -3 to 3
- ln_gain: float32 [128], replicated, may hold values from 0.25 to 1.75
- ln_bias: float32 [128], replicated, may hold values from -3 to 3
- w_up: bfloat16 [128, 512], replicated, may hold values from -0.5 to 0.5
- up_bias: float32 [512], replicated, may hold values from -3 to 3
- w_down: bfloat16 [512, 128], replicated, may hold values from -0.25 to 0.25
- down_bias: float32 [128], replicated, may hold values from -3 to 3
- layer_scale: float32 [128], replicated, may hold values from 0.3 to 1
Outputs:
- grad_fields: bfloat16 [4, 64, 64, 64, 128], P('dp', 'tile')
- g_kernel: float32 [7, 7, 128], replicated
- g_conv_bias: float32 [128], replicated
- g_ln_gain: float32 [128], replicated
- g_ln_bias: float32 [128], replicated
- g_w_up: float32 [128, 512], replicated
- g_up_bias: float32 [512], replicated
- g_w_down: float32 [512, 128], replicated
- g_down_bias: float32 [128], replicated
- g_layer_scale: float32 [128], replicated
Inputs may be any that keep to these rules, and one draw needn't show every extreme that they name: `is_ocean`: slots follow a serpentine curve through the columns of a grid of 8 x 8 tiles, alternating direction from column to column; tiles of the first and last grid rows are ocean. Entry k of slot s names the slot of the tile adjacent in direction k (north, south, west, east, north-west, north-east, south-west, south-east), or -1 where that tile is land or outside the grid or slot s is land; the relation is symmetric; the north and south neighbours are slot s - 1 or s + 1, and every neighbour lies within 15 slots of s.
All inputs are finite; a program needn't handle non-finite values.
Results may differ from a plain program's by a relative error of at most 0.0071.
Values may be sent and summed in bfloat16 or wider, within the bound.
No kernel may reach another device: no remote copies, remote signals or barrier semaphores. Data moves between devices by JAX's collectives and lax.ppermute only.
A program may use at most 128 MiB of HBM per device.

v0:
```python
from functools import partial
import math
import jax
import jax.numpy as jnp
from jax import lax
from jax.sharding import PartitionSpec as P

TROWS = 8
EPSILON = 1e-06


def passed_along(value, axis, by):
    devices = lax.axis_size(axis)
    pairs = [(i, i + by) for i in range(devices) if 0 <= i + by < devices]
    return lax.ppermute(value, axis, pairs)


def rims_of(tile_block, rim_depth):
    extent = tile_block.shape[0]
    top_band = tile_block[:rim_depth]
    bottom = tile_block[extent - rim_depth :]
    left_band = jnp.transpose(tile_block[:, :rim_depth], (1, 0, 2))
    right_band = jnp.transpose(tile_block[:, extent - rim_depth :], (1, 0, 2))
    return jnp.stack([top_band, bottom, left_band, right_band], 0)


def assemble(own_tile, picked, valid_flags, first_layer, rim_depth):
    extent = own_tile.shape[0]

    def rim_piece(direction, which_strip):
        stripe = picked[direction][which_strip, first_layer : first_layer + rim_depth]
        return stripe * valid_flags[direction].astype(own_tile.dtype)

    north_rim = rim_piece(0, 1)
    south_rim = rim_piece(1, 0)
    west_rim = jnp.transpose(rim_piece(2, 1), (1, 0, 2))
    east_rim = jnp.transpose(rim_piece(3, 0), (1, 0, 2))
    north_west = jnp.transpose(rim_piece(4, 1)[:, extent - rim_depth :], (1, 0, 2))
    north_east = jnp.transpose(rim_piece(5, 0)[:, extent - rim_depth :], (1, 0, 2))
    south_west = jnp.transpose(rim_piece(6, 1)[:, :rim_depth], (1, 0, 2))
    south_east = jnp.transpose(rim_piece(7, 0)[:, :rim_depth], (1, 0, 2))
    top_band = jnp.concatenate([north_west, north_rim, north_east], 1)
    middle = jnp.concatenate([west_rim, own_tile, east_rim], 1)
    bottom = jnp.concatenate([south_west, south_rim, south_east], 1)
    return jnp.concatenate([top_band, middle, bottom], 0)


def depthwise(padded, kernel, extent):
    running_sum = jnp.zeros((extent, extent, padded.shape[2]), jnp.float32)
    for lag_row in range(7):
        for lag_col in range(7):
            window = padded[lag_row : lag_row + extent, lag_col : lag_col + extent].astype(
                jnp.float32
            )
            running_sum = running_sum + window * kernel[lag_row, lag_col]
    return running_sum


def transposed(grad_padded, kernel, extent):
    running_sum = jnp.zeros((extent, extent, grad_padded.shape[2]), jnp.float32)
    for lag_row in range(7):
        for lag_col in range(7):
            window = grad_padded[
                6 - lag_row : 6 - lag_row + extent, 6 - lag_col : 6 - lag_col + extent
            ].astype(jnp.float32)
            running_sum = running_sum + window * kernel[lag_row, lag_col]
    return running_sum


def kernel_terms(grad_tile, padded, extent):
    grad_values = grad_tile.astype(jnp.float32)
    stacked = []
    for lag_row in range(7):
        line_terms = []
        for lag_col in range(7):
            window = padded[lag_row : lag_row + extent, lag_col : lag_col + extent].astype(
                jnp.float32
            )
            line_terms.append(jnp.sum(grad_values * window, axis=(0, 1)))
        stacked.append(jnp.stack(line_terms, 0))
    return jnp.stack(stacked, 0)


def gelu_tanh(values):
    return jax.nn.gelu(values, approximate=True)


def contract_last(left_rows, right_matrix):
    return lax.dot_general(
        left_rows, right_matrix, (((1,), (1,)), ((), ())), preferred_element_type=jnp.float32
    )


def contract_first(left_rows, right_rows):
    return lax.dot_general(
        left_rows, right_rows, (((0,), (0,)), ((), ())), preferred_element_type=jnp.float32
    )


def layer_rows(
    conv_rows, cot_rows, ln_gain, ln_bias, w_up, up_bias, w_down, down_bias, layer_scale
):
    mean_value = jnp.mean(conv_rows, -1, keepdims=True)
    centred = conv_rows - mean_value
    variance = jnp.mean(centred * centred, -1, keepdims=True)
    inverse_scale = lax.rsqrt(variance + EPSILON)
    normed = centred * inverse_scale
    scaled = (normed * ln_gain + ln_bias).astype(jnp.bfloat16)
    hidden_sum = jnp.dot(scaled, w_up, preferred_element_type=jnp.float32) + up_bias
    activation = gelu_tanh(hidden_sum).astype(jnp.bfloat16)
    mixed = jnp.dot(activation, w_down, preferred_element_type=jnp.float32) + down_bias
    grad_mixed = (cot_rows * layer_scale).astype(jnp.bfloat16)
    grad_act = contract_last(grad_mixed, w_down)
    pullback = jax.vjp(gelu_tanh, hidden_sum)[1]
    grad_pre = pullback(grad_act)[0].astype(jnp.bfloat16)
    grad_scaled = contract_last(grad_pre, w_up)
    grad_normed = grad_scaled * ln_gain
    grad_conv = inverse_scale * (
        grad_normed
        - jnp.mean(grad_normed, -1, keepdims=True)
        - normed * jnp.mean(grad_normed * normed, -1, keepdims=True)
    )
    return (
        grad_conv.astype(jnp.bfloat16),
        mixed,
        grad_mixed,
        activation,
        grad_pre,
        scaled,
        grad_scaled,
        normed,
    )


def row_terms(
    cot_rows, mixed, grad_mixed, activation, grad_pre, scaled, grad_scaled, normed, grad_conv
):
    return (
        jnp.sum(grad_conv.astype(jnp.float32), 0),
        jnp.sum(grad_scaled * normed, 0),
        jnp.sum(grad_scaled, 0),
        contract_first(scaled, grad_pre),
        jnp.sum(grad_pre.astype(jnp.float32), 0),
        contract_first(activation, grad_mixed),
        jnp.sum(grad_mixed.astype(jnp.float32), 0),
        jnp.sum(cot_rows * mixed, 0),
    )


def local(
    fields,
    cotangent,
    is_ocean,
    neighbours,
    kernel,
    conv_bias,
    ln_gain,
    ln_bias,
    w_up,
    up_bias,
    w_down,
    down_bias,
    layer_scale,
):
    samples, slot_count, extent, channels = (
        fields.shape[0],
        fields.shape[1],
        fields.shape[2],
        fields.shape[4],
    )
    hidden_width = w_up.shape[1]
    tile_count = lax.axis_size("tile")
    reach_span = min((2 * TROWS + slot_count - 2) // slot_count, tile_count - 1)
    position = lax.axis_index("tile")
    vert_base = (position - 1) * slot_count
    side_base = (position - reach_span) * slot_count
    layer_params = (ln_gain, ln_bias, w_up, up_bias, w_down, down_bias, layer_scale)
    zero_terms = (
        jnp.zeros((7, 7, channels), jnp.float32),
        jnp.zeros((channels,), jnp.float32),
        jnp.zeros((channels,), jnp.float32),
        jnp.zeros((channels,), jnp.float32),
        jnp.zeros((channels, hidden_width), jnp.float32),
        jnp.zeros((hidden_width,), jnp.float32),
        jnp.zeros((hidden_width, channels), jnp.float32),
        jnp.zeros((channels,), jnp.float32),
        jnp.zeros((channels,), jnp.float32),
    )

    def collect(rim_set):
        adjacent = {}
        for offset in (1, -1):
            adjacent[offset] = passed_along(rim_set, "tile", offset)
        vertical = jnp.concatenate([adjacent[1], rim_set, adjacent[-1]], 1)
        distant = {}
        for distance in range(2, reach_span + 1):
            for offset in (distance, -distance):
                distant[offset] = passed_along(rim_set, "tile", offset)[:, :, 2:4]
        below_list = [distant[distance] for distance in range(reach_span, 1, -1)]
        above_list = [distant[-distance] for distance in range(2, reach_span + 1)]
        middle_list = [adjacent[1][:, :, 2:4], rim_set[:, :, 2:4], adjacent[-1][:, :, 2:4]]
        sideways = jnp.concatenate(below_list + middle_list + above_list, 1)
        bases = jnp.zeros((6,), jnp.int32) + side_base
        return (vertical, sideways, bases)

    def fetch_rims(vertical, sideways, bases, slot_ids):
        upright = jnp.clip(slot_ids[:2] - vert_base, 0, vertical.shape[0] - 1)
        lateral = jnp.clip(slot_ids[2:] - bases, 0, sideways.shape[0] - 1)
        picked = [vertical[upright[0]], vertical[upright[1]]]
        picked = picked + [sideways[lateral[slot_pick]] for slot_pick in range(6)]
        return (picked, slot_ids >= 0)

    grad_sums = zero_terms
    rims_x = jax.vmap(jax.vmap(partial(rims_of, rim_depth=3)))(fields)
    vertical_x, sideways_x, bases_x = collect(rims_x)
    sample = 0
    tile_stack = fields[sample]
    cot_stack = cotangent[sample]

    def first_work(slot_id):
        picked, valid_flags = fetch_rims(
            vertical_x[sample], sideways_x[sample], bases_x, neighbours[slot_id]
        )
        padded = assemble(tile_stack[slot_id], picked, valid_flags, 0, 3)
        conv_out = depthwise(padded, kernel, extent) + conv_bias
        cot_rows = cot_stack[slot_id].astype(jnp.float32).reshape(-1, channels)
        layer_parts = layer_rows(conv_out.reshape(-1, channels), cot_rows, *layer_params)
        grad_tile = layer_parts[0].reshape(extent, extent, channels)
        weight_terms = (kernel_terms(grad_tile, padded, extent),) + row_terms(
            cot_rows, *layer_parts[1:], layer_parts[0]
        )
        keep_flag = (is_ocean[slot_id] > 0).astype(jnp.float32)
        return (grad_tile, tuple((keep_flag * term for term in weight_terms)))

    def first_step(running, slot_id):
        grad_tile, weight_terms = first_work(slot_id)
        return (tuple((total + term for total, term in zip(running, weight_terms))), grad_tile)

    grad_sums, sample_grads = lax.scan(first_step, grad_sums, jnp.arange(slot_count))
    grad_tiles = [sample_grads]
    grad_stack = jnp.stack(grad_tiles, 0)
    rims_g = jax.vmap(jax.vmap(partial(rims_of, rim_depth=3)))(grad_stack)
    vertical_g, sideways_g, bases_g = collect(rims_g)
    sample = 0
    cot_stack = cotangent[sample]

    def second_step(slot_id):
        picked, valid_flags = fetch_rims(
            vertical_g[sample], sideways_g[sample], bases_g, neighbours[slot_id]
        )
        grad_padded = assemble(grad_stack[sample, slot_id], picked, valid_flags, 0, 3)
        result = cot_stack[slot_id].astype(jnp.float32) + transposed(grad_padded, kernel, extent)
        keep_flag = (is_ocean[slot_id] > 0).astype(jnp.float32)
        return (result * keep_flag).astype(jnp.bfloat16)

    outputs = [lax.map(second_step, jnp.arange(slot_count))]
    summed = lax.psum(
        (
            grad_sums[0],
            grad_sums[1],
            grad_sums[2],
            grad_sums[3],
            grad_sums[4],
            grad_sums[5],
            grad_sums[6],
            grad_sums[7],
            grad_sums[8],
        ),
        ("tile", "dp"),
    )
    grad_scale = 1.0 / math.sqrt(
        samples * lax.axis_size("dp") * slot_count * tile_count * extent * extent
    )
    return (
        jnp.stack(outputs, 0),
        summed[0] * grad_scale,
        summed[1] * grad_scale,
        summed[2] * grad_scale,
        summed[3] * grad_scale,
        summed[4] * grad_scale,
        summed[5] * grad_scale,
        summed[6] * grad_scale,
        summed[7] * grad_scale,
        summed[8] * grad_scale,
    )


def solution(mesh):
    placed = (
        P("dp", "tile", None, None, None),
        P("dp", "tile", None, None, None),
        P("tile"),
        P("tile", None),
        P(),
        P(),
        P(),
        P(),
        P(),
        P(),
        P(),
        P(),
        P(),
    )
    return jax.shard_map(
        local,
        mesh=mesh,
        in_specs=placed,
        out_specs=(P("dp", "tile", None, None, None), P(), P(), P(), P(), P(), P(), P(), P(), P()),
        check_vma=False,
    )
```

profile of v0, /device:TPU:1, one launch (start us, length us, event | category | flops | bytes accessed | tf_op | source)
XLA Modules:
  0.0 865.7 jit_solution(16494934024993436842)
XLA Ops:
  17.4 5.7 collective-permute-start.2
  25.1 5.1 collective-permute-start.4
  35.7 13.1 %collective-permute-done.2 = bf16[1,2,4,3,64,128]{5,4,3,2,1,0:T(8,128)(2,1)S(1)} collective-permute-done((bf16[1,2,4,3,64,128]{5,4,3,2,1,0:T(8,128)(2,1)S(1)}, bf16[1,2,4,3,64,128]{5,4,3,2,1,0:T(8,128)(2,1)S(1)}, u32[]{:S(2)}, u32[]{:S(2)}) %collective-permute-start.2) | collective-permute-done | bytes 393248 | tf_op jit(solution)/shard_map/ppermute | solution.py:15
  73.0 4.9 collective-permute-done.11
  77.9 10.7 %collective-permute-done.12 = bf16[1,2,4,3,64,128]{5,4,3,2,1,0:T(8,128)(2,1)S(1)} collective-permute-done((bf16[1,2,4,3,64,128]{5,4,3,2,1,0:T(8,128)(2,1)S(1)}, bf16[1,2,4,3,64,128]{5,4,3,2,1,0:T(8,128)(2,1)S(1)}, u32[]{:S(2)}, u32[]{:S(2)}) %collective-permute-start.12) | collective-permute-done | bytes 393248 | tf_op jit(solution)/shard_map/ppermute | solution.py:15
  88.6 8.4 collective-permute-done.13
  97.0 22.3 %collective-permute-done.14 = bf16[1,2,4,3,64,128]{5,4,3,2,1,0:T(8,128)(2,1)S(1)} collective-permute-done((bf16[1,2,4,3,64,128]{5,4,3,2,1,0:T(8,128)(2,1)S(1)}, bf16[1,2,4,3,64,128]{5,4,3,2,1,0:T(8,128)(2,1)S(1)}, u32[]{:S(2)}, u32[]{:S(2)}) %collective-permute-start.14) | collective-permute-done | bytes 393248 | tf_op jit(solution)/shard_map/ppermute | solution.py:15
  121.0 6.8 copy.25
  130.9 242.7 %while.43 = (s32[]{:T(128)}, f32[7,7,128]{2,1,0:T(8,128)}, f32[128]{0:T(128)}, f32[128]{0:T(128)}, f32[128]{0:T(128)}, /*index=5*/f32[128,512]{1,0:T(8,128)}, f3...) while((s32[]{:T(128)}, f32[7,7,128]{2,1,0:T(8,128)}, ...), condition=%wide.region_60.61_spmd.clone, body=%wide.region_0.60_spmd.clone.sunk | while | flops 3501007360 | bytes 273028160 | solution.py:239
  177.4 16.3 %fusion.232 = (f32[64,64]{1,0:T(8,128)S(1)}, f32[64,64,128]{2,1,0:T(8,128)S(1)}) fusion(f32[128]{0:T(128)S(1)} %get-tuple-element.1736, f32[128]{0:T(128)S(1)} %get-tuple-element.1527, bf16[67,70,128]{2,1,0:T(8,128)(2,1)S(1)} %get-tuple-element.1526, f32[128]{0:T(128)S(1)} %get-tuple-element.1528, f32[128]{0:T(128)S(1)} %get-tuple-element.1529, ...), kind=kLoop, calls=%fused_computation.494.clone.1 | loop fusion | flops 87027712 | bytes 47326208 | tf_op jit(solution)/shard_map/while/body/eval_jaxpr/reduce_sum | solution.py:103
  203.8 7.3 convert_reduce_fusion.6
  214.1 9.7 %fusion.234 = (f32[128]{0:T(128)}, f32[128]{0:T(128)}, f32[128]{0:T(128)}, f32[128]{0:T(128)}, f32[128]{0:T(128)}, /*index=5*/f32[128]{0:T(128)}, f32[128]{0:T(1...) fusion(bf16[67,70,128]{2,1,0:T(8,128)(2,1)S(1)} %get-tuple-elem, ...), kind=kLoop, calls=%fused_computation.301.clone.1 | loop fusion | flops 33027840 | bytes 24192512 | tf_op jit(solution)/shard_map/while/body/eval_jaxpr/reduce_sum | solution.py:79
  237.3 8.7 %fusion.235 = (f32[128]{0:T(128)}, f32[128]{0:T(128)}, f32[128]{0:T(128)}, f32[128]{0:T(128)}, f32[128]{0:T(128)}, /*index=5*/f32[128]{0:T(128)}, f32[128]{0:T(1...) fusion(bf16[67,70,128]{2,1,0:T(8,128)(2,1)S(1)} %get-tuple-element.1526, ...), kind=kLoop, calls=%fused_computation.283.clone.1 | loop fusion | flops 28834304 | bytes 8493056 | tf_op jit(solution)/shard_map/while/body/eval_jaxpr/reduce_sum | solution.py:79
  247.5 5.2 fusion.236
  291.5 16.3 %fusion.232 = (f32[64,64]{1,0:T(8,128)S(1)}, f32[64,64,128]{2,1,0:T(8,128)S(1)}) fusion(f32[128]{0:T(128)S(1)} %get-tuple-element.1736, f32[128]{0:T(128)S(1)} %get-tuple-element.1527, bf16[67,70,128]{2,1,0:T(8,128)(2,1)S(1)} %get-tuple-element.1526, f32[128]{0:T(128)S(1)} %get-tuple-element.1528, f32[128]{0:T(128)S(1)} %get-tuple-element.1529, ...), kind=kLoop, calls=%fused_computation.494.clone.1 | loop fusion | flops 87027712 | bytes 47326208 | tf_op jit(solution)/shard_map/while/body/eval_jaxpr/reduce_sum | solution.py:103
  317.8 7.3 convert_reduce_fusion.6
  328.1 9.7 %fusion.234 = (f32[128]{0:T(128)}, f32[128]{0:T(128)}, f32[128]{0:T(128)}, f32[128]{0:T(128)}, f32[128]{0:T(128)}, /*index=5*/f32[128]{0:T(128)}, f32[128]{0:T(1...) fusion(bf16[67,70,128]{2,1,0:T(8,128)(2,1)S(1)} %get-tuple-elem, ...), kind=kLoop, calls=%fused_computation.301.clone.1 | loop fusion | flops 33027840 | bytes 24192512 | tf_op jit(solution)/shard_map/while/body/eval_jaxpr/reduce_sum | solution.py:79
  351.3 8.7 %fusion.235 = (f32[128]{0:T(128)}, f32[128]{0:T(128)}, f32[128]{0:T(128)}, f32[128]{0:T(128)}, f32[128]{0:T(128)}, /*index=5*/f32[128]{0:T(128)}, f32[128]{0:T(1...) fusion(bf16[67,70,128]{2,1,0:T(8,128)(2,1)S(1)} %get-tuple-element.1526, ...), kind=kLoop, calls=%fused_computation.283.clone.1 | loop fusion | flops 28834304 | bytes 8493056 | tf_op jit(solution)/shard_map/while/body/eval_jaxpr/reduce_sum | solution.py:79
  361.5 5.2 fusion.236
  369.0 4.3 fusion.240
  376.5 6.5 collective-permute-start.23
  389.0 6.0 collective-permute-start.17
  396.4 82.6 %all-reduce = (f32[7,7,128]{2,1,0:T(8,128)S(1)}, f32[128]{0:T(128)S(1)}, f32[128]{0:T(128)S(1)}, f32[128]{0:T(128)S(1)}, f32[512]{0:T(512)S(1)}, /*index=5*/f32[128]{0:T(128)S(1)}, f32[128]{0:T(128)S(1)}) all-reduce(f32[7,7,128]{2,1,0:T(8,128)S(1)} %copy-done.21, ...), channel_id=1, replica_groups=mesh['tile'=32,'dp'=4] {'tile','dp'}, use_global_device_ids=true, to_apply=%region_63.64 | all-reduce | flops 7424 | bytes 59392 | tf_op jit(solution)/shard_map/psum | solution.py:257
  482.8 142.8 %all-reduce.4.cloned.1.call-done = (f32[128,512]{1,0:T(8,128)}, f32[512,128]{1,0:T(8,128)}) async-done(((f32[128,512]{1,0:T(8,128)}, f32[512,128]{1,0:T(8,128)}), (f32[128,512]{1,0:T(8,128)}, f32[512,128]{1,0:T(8,128)})) %all-reduce.4.cloned.1.call-update) | async-done | bytes 524304 | tf_op jit(solution)/shard_map/psum | solution.py:257
  636.9 6.0 collective-permute-start.21
  649.0 34.7 %collective-permute-done.19 = bf16[1,2,4,3,64,128]{5,3,4,1,0,2:T(4,128)(2,1)S(1)} collective-permute-done((bf16[1,2,4,3,64,128]{5,3,4,1,0,2:T(4,128)(2,1)S(1)}, bf16[1,2,4,3,64,128]{5,3,4,1,0,2:T(4,128)(2,1)S(1)}, u32[]{:S(2)}, u32[]{:S(2)}) %collective-permute-start.19) | collective-permute-done | bytes 393248 | tf_op jit(solution)/shard_map/ppermute | solution.py:15
  693.0 18.9 %collective-permute-done.26 = bf16[1,2,4,3,64,128]{5,3,4,1,0,2:T(4,128)(2,1)S(1)} collective-permute-done((bf16[1,2,4,3,64,128]{5,3,4,1,0,2:T(4,128)(2,1)S(1)}, bf16[1,2,4,3,64,128]{5,3,4,1,0,2:T(4,128)(2,1)S(1)}, u32[]{:S(2)}, u32[]{:S(2)}) %collective-permute-start.26) | collective-permute-done | bytes 393248 | tf_op jit(solution)/shard_map/ppermute | solution.py:15
  716.0 22.6 %collective-permute-done.30 = bf16[1,2,4,3,64,128]{5,3,4,1,0,2:T(4,128)(2,1)S(1)} collective-permute-done((bf16[1,2,4,3,64,128]{5,3,4,1,0,2:T(4,128)(2,1)S(1)}, bf16[1,2,4,3,64,128]{5,3,4,1,0,2:T(4,128)(2,1)S(1)}, u32[]{:S(2)}, u32[]{:S(2)}) %collective-permute-start.30) | collective-permute-done | bytes 393248 | tf_op jit(solution)/shard_map/ppermute | solution.py:15
  738.7 14.6 %collective-permute-done.31 = bf16[1,2,4,3,64,128]{5,3,4,1,0,2:T(4,128)(2,1)S(1)} collective-permute-done((bf16[1,2,4,3,64,128]{5,3,4,1,0,2:T(4,128)(2,1)S(1)}, bf16[1,2,4,3,64,128]{5,3,4,1,0,2:T(4,128)(2,1)S(1)}, u32[]{:S(2)}, u32[]{:S(2)}) %collective-permute-start.31) | collective-permute-done | bytes 393248 | tf_op jit(solution)/shard_map/ppermute | solution.py:15
  759.3 99.1 %while.42 = (s32[]{:T(128)}, bf16[2,64,64,128]{3,2,1,0:T(8,128)(2,1)}, s32[2]{0:T(128)S(1)}, bf16[2,64,64,128]{3,2,1,0:T(8,128)(2,1)S(1)}, s32[2,8]{1,0:T(2,128)...) while((s32[]{:T(128)}, ...), condition=%wide.region_62.63_spmd.clone, body=%wide.region_61.62_spmd.clone.sunk | while | flops 102684736 | bytes 53919052 | solution.py:256
  792.3 16.7 %bitcast_dynamic-update-slice_fusion.2 = bf16[2,64,64,128]{3,2,1,0:T(8,128)(2,1)} fusion(bf16[2,64,64,128]{3,2,1,0:T(8,128)(2,1)} %get-tuple-element.1773, s32[]{:T(128)} %get-tuple-element.1772, f32[]{:T(128)} %bitcast.632, f32[128]{0:T(128)S(1)} %get-tuple-element.1390, bf16[67,70,128]{2,1,0:T(8,128)(2,1)S(1)} %get-tuple-element.1421, ...), kind=kLoop, calls=%fused_computation.21.clone.1 | loop fusion | flops 88080384 | bytes 47310340 | tf_op jit(solution)/shard_map/while/body/jit(dynamic_update_index_in_dim)/dynamic_update_slice | solution.py:239
  841.7 16.7 %bitcast_dynamic-update-slice_fusion.2 = bf16[2,64,64,128]{3,2,1,0:T(8,128)(2,1)} fusion(bf16[2,64,64,128]{3,2,1,0:T(8,128)(2,1)} %get-tuple-element.1773, s32[]{:T(128)} %get-tuple-element.1772, f32[]{:T(128)} %bitcast.632, f32[128]{0:T(128)S(1)} %get-tuple-element.1390, bf16[67,70,128]{2,1,0:T(8,128)(2,1)S(1)} %get-tuple-element.1421, ...), kind=kLoop, calls=%fused_computation.21.clone.1 | loop fusion | flops 88080384 | bytes 47310340 | tf_op jit(solution)/shard_map/while/body/jit(dynamic_update_index_in_dim)/dynamic_update_slice | solution.py:239
  (526 shorter events, 196.6 us)
Async XLA Ops:
  7.2 618.5 %all-reduce.4.cloned.1.call-start = ((), (), s32[]{:S(2)}) async-start(), calls=%async_computation | async-start | bytes 1048576 | tf_op jit(solution)/shard_map/psum | solution.py:257
  9.4 20.9 %collective-permute-start = (bf16[1,2,4,3,64,128]{5,4,3,2,1,0:T(8,128)(2,1)S(1)}, bf16[1,2,4,3,64,128]{5,4,3,2,1,0:T(8,128)(2,1)S(1)}, u32[]{:S(2)}, u32[]{:S(2)}) collective-permute-start(bf16[1,2,4,3,64,128]{5,4,3,2,1,0:T(8,128)(2,1)S(1)} %maximum_bitcast_fusion.1), channel_id=1, source_target_pairs={{0,32},{4,36},{8,40},{12,44},{16,48},{20,52},{24,56},{28,60},{32,6... | collective-permute-start | bytes 1179656 | tf_op jit(solution)/shard_map/ppermute | solution.py:15
  13.4 19.5 %collective-permute-start.1 = (bf16[1,2,4,3,64,128]{5,4,3,2,1,0:T(8,128)(2,1)S(1)}, bf16[1,2,4,3,64,128]{5,4,3,2,1,0:T(8,128)(2,1)S(1)}, u32[]{:S(2)}, u32[]{:S(2)}) collective-permute-start(bf16[1,2,4,3,64,128]{5,4,3,2,1,0:T(8,128)(2,1)S(1)} %maximum_bitcast_fusion.1), channel_id=1, source_target_pairs={{0,28},{4,32},{8,36},{12,40},{16,44},{20,48},{24,52},{28,56},{32,6... | collective-permute-start | bytes 1179656 | tf_op jit(solution)/shard_map/ppermute | solution.py:15
  17.4 31.4 %collective-permute-start.2 = (bf16[1,2,4,3,64,128]{5,4,3,2,1,0:T(8,128)(2,1)S(1)}, bf16[1,2,4,3,64,128]{5,4,3,2,1,0:T(8,128)(2,1)S(1)}, u32[]{:S(2)}, u32[]{:S(2)}) collective-permute-start(bf16[1,2,4,3,64,128]{5,4,3,2,1,0:T(8,128)(2,1)S(1)} %maximum_bitcast_fusion.1), channel_id=1, source_target_pairs={{0,24},{4,28},{8,32},{12,36},{16,40},{20,44},{24,48},{28,52},{32,5... | collective-permute-start | bytes 1179656 | tf_op jit(solution)/shard_map/ppermute | solution.py:15
  23.0 30.8 %collective-permute-start.3 = (bf16[1,2,4,3,64,128]{5,4,3,2,1,0:T(8,128)(2,1)S(1)}, bf16[1,2,4,3,64,128]{5,4,3,2,1,0:T(8,128)(2,1)S(1)}, u32[]{:S(2)}, u32[]{:S(2)}) collective-permute-start(bf16[1,2,4,3,64,128]{5,4,3,2,1,0:T(8,128)(2,1)S(1)} %maximum_bitcast_fusion.1), channel_id=1, source_target_pairs={{0,20},{4,24},{8,28},{12,32},{16,36},{20,40},{24,44},{28,48},{32,5... | collective-permute-start | bytes 1179656 | tf_op jit(solution)/shard_map/ppermute | solution.py:15
  25.1 30.7 %collective-permute-start.4 = (bf16[1,2,4,3,64,128]{5,4,3,2,1,0:T(8,128)(2,1)S(1)}, bf16[1,2,4,3,64,128]{5,4,3,2,1,0:T(8,128)(2,1)S(1)}, u32[]{:S(2)}, u32[]{:S(2)}) collective-permute-start(bf16[1,2,4,3,64,128]{5,4,3,2,1,0:T(8,128)(2,1)S(1)} %maximum_bitcast_fusion.1), channel_id=1, source_target_pairs={{0,16},{4,20},{8,24},{12,28},{16,32},{20,36},{24,40},{28,44},{32,4... | collective-permute-start | bytes 1179656 | tf_op jit(solution)/shard_map/ppermute | solution.py:15
  30.3 26.8 %collective-permute-start.5 = (bf16[1,2,4,3,64,128]{5,4,3,2,1,0:T(8,128)(2,1)S(1)}, bf16[1,2,4,3,64,128]{5,4,3,2,1,0:T(8,128)(2,1)S(1)}, u32[]{:S(2)}, u32[]{:S(2)}) collective-permute-start(bf16[1,2,4,3,64,128]{5,4,3,2,1,0:T(8,128)(2,1)S(1)} %maximum_bitcast_fusion.1), channel_id=1, source_target_pairs={{0,12},{4,16},{8,20},{12,24},{16,28},{20,32},{24,36},{28,40},{32,4... | collective-permute-start | bytes 1179656 | tf_op jit(solution)/shard_map/ppermute | solution.py:15
  32.9 25.5 %collective-permute-start.6 = (bf16[1,2,4,3,64,128]{5,4,3,2,1,0:T(8,128)(2,1)S(1)}, bf16[1,2,4,3,64,128]{5,4,3,2,1,0:T(8,128)(2,1)S(1)}, u32[]{:S(2)}, u32[]{:S(2)}) collective-permute-start(bf16[1,2,4,3,64,128]{5,4,3,2,1,0:T(8,128)(2,1)S(1)} %maximum_bitcast_fusion.1), channel_id=1, source_target_pairs={{0,8},{4,12},{8,16},{12,20},{16,24},{20,28},{24,32},{28,36},{32,40... | collective-permute-start | bytes 1179656 | tf_op jit(solution)/shard_map/ppermute | solution.py:15
  53.8 11.9 %collective-permute-start.8 = (bf16[1,2,4,3,64,128]{5,4,3,2,1,0:T(8,128)(2,1)S(1)}, bf16[1,2,4,3,64,128]{5,4,3,2,1,0:T(8,128)(2,1)S(1)}, u32[]{:S(2)}, u32[]{:S(2)}) collective-permute-start(bf16[1,2,4,3,64,128]{5,4,3,2,1,0:T(8,128)(2,1)S(1)} %maximum_bitcast_fusion.1), channel_id=1, source_target_pairs={{4,0},{8,4},{12,8},{16,12},{20,16},{24,20},{28,24},{32,28},{36,32}... | collective-permute-start | bytes 1179656 | tf_op jit(solution)/shard_map/ppermute | solution.py:15
  55.8 13.0 %collective-permute-start.9 = (bf16[1,2,4,3,64,128]{5,4,3,2,1,0:T(8,128)(2,1)S(1)}, bf16[1,2,4,3,64,128]{5,4,3,2,1,0:T(8,128)(2,1)S(1)}, u32[]{:S(2)}, u32[]{:S(2)}) collective-permute-start(bf16[1,2,4,3,64,128]{5,4,3,2,1,0:T(8,128)(2,1)S(1)} %maximum_bitcast_fusion.1), channel_id=1, source_target_pairs={{8,0},{12,4},{16,8},{20,12},{24,16},{28,20},{32,24},{36,28},{40,32... | collective-permute-start | bytes 1179656 | tf_op jit(solution)/shard_map/ppermute | solution.py:15
  57.2 14.5 %collective-permute-start.10 = (bf16[1,2,4,3,64,128]{5,4,3,2,1,0:T(8,128)(2,1)S(1)}, bf16[1,2,4,3,64,128]{5,4,3,2,1,0:T(8,128)(2,1)S(1)}, u32[]{:S(2)}, u32[]{:S(2)}) collective-permute-start(bf16[1,2,4,3,64,128]{5,4,3,2,1,0:T(8,128)(2,1)S(1)} %maximum_bitcast_fusion.1), channel_id=1, source_target_pairs={{12,0},{16,4},{20,8},{24,12},{28,16},{32,20},{36,24},{40,28},{44,3... | collective-permute-start | bytes 1179656 | tf_op jit(solution)/shard_map/ppermute | solution.py:15
  58.5 19.3 %collective-permute-start.11 = (bf16[1,2,4,3,64,128]{5,4,3,2,1,0:T(8,128)(2,1)S(1)}, bf16[1,2,4,3,64,128]{5,4,3,2,1,0:T(8,128)(2,1)S(1)}, u32[]{:S(2)}, u32[]{:S(2)}) collective-permute-start(bf16[1,2,4,3,64,128]{5,4,3,2,1,0:T(8,128)(2,1)S(1)} %maximum_bitcast_fusion.1), channel_id=1, source_target_pairs={{16,0},{20,4},{24,8},{28,12},{32,16},{36,20},{40,24},{44,28},{48,3... | collective-permute-start | bytes 1179656 | tf_op jit(solution)/shard_map/ppermute | solution.py:15
  60.2 28.4 %collective-permute-start.12 = (bf16[1,2,4,3,64,128]{5,4,3,2,1,0:T(8,128)(2,1)S(1)}, bf16[1,2,4,3,64,128]{5,4,3,2,1,0:T(8,128)(2,1)S(1)}, u32[]{:S(2)}, u32[]{:S(2)}) collective-permute-start(bf16[1,2,4,3,64,128]{5,4,3,2,1,0:T(8,128)(2,1)S(1)} %maximum_bitcast_fusion.1), channel_id=1, source_target_pairs={{20,0},{24,4},{28,8},{32,12},{36,16},{40,20},{44,24},{48,28},{52,3... | collective-permute-start | bytes 1179656 | tf_op jit(solution)/shard_map/ppermute | solution.py:15
  65.7 31.3 %collective-permute-start.13 = (bf16[1,2,4,3,64,128]{5,4,3,2,1,0:T(8,128)(2,1)S(1)}, bf16[1,2,4,3,64,128]{5,4,3,2,1,0:T(8,128)(2,1)S(1)}, u32[]{:S(2)}, u32[]{:S(2)}) collective-permute-start(bf16[1,2,4,3,64,128]{5,4,3,2,1,0:T(8,128)(2,1)S(1)} %maximum_bitcast_fusion.1), channel_id=1, source_target_pairs={{24,0},{28,4},{32,8},{36,12},{40,16},{44,20},{48,24},{52,28},{56,3... | collective-permute-start | bytes 1179656 | tf_op jit(solution)/shard_map/ppermute | solution.py:15
  68.8 50.5 %collective-permute-start.14 = (bf16[1,2,4,3,64,128]{5,4,3,2,1,0:T(8,128)(2,1)S(1)}, bf16[1,2,4,3,64,128]{5,4,3,2,1,0:T(8,128)(2,1)S(1)}, u32[]{:S(2)}, u32[]{:S(2)}) collective-permute-start(bf16[1,2,4,3,64,128]{5,4,3,2,1,0:T(8,128)(2,1)S(1)} %maximum_bitcast_fusion.1), channel_id=1, source_target_pairs={{28,0},{32,4},{36,8},{40,12},{44,16},{48,20},{52,24},{56,28},{60,3... | collective-permute-start | bytes 1179656 | tf_op jit(solution)/shard_map/ppermute | solution.py:15
  71.6 49.3 %collective-permute-start.15 = (bf16[1,2,4,3,64,128]{5,4,3,2,1,0:T(8,128)(2,1)S(1)}, bf16[1,2,4,3,64,128]{5,4,3,2,1,0:T(8,128)(2,1)S(1)}, u32[]{:S(2)}, u32[]{:S(2)}) collective-permute-start(bf16[1,2,4,3,64,128]{5,4,3,2,1,0:T(8,128)(2,1)S(1)} %maximum_bitcast_fusion.1), channel_id=1, source_target_pairs={{32,0},{36,4},{40,8},{44,12},{48,16},{52,20},{56,24},{60,28},{64,3... | collective-permute-start | bytes 1179656 | tf_op jit(solution)/shard_map/ppermute | solution.py:15
  376.5 252.5 %collective-permute-start.23 = (bf16[1,2,4,3,64,128]{5,3,4,1,0,2:T(4,128)(2,1)S(1)}, bf16[1,2,4,3,64,128]{5,3,4,1,0,2:T(4,128)(2,1)S(1)}, u32[]{:S(2)}, u32[]{:S(2)}) collective-permute-start(bf16[1,2,4,3,64,128]{5,3,4,1,0,2:T(4,128)(2,1)S(1)} %maximum_bitcast_fusion), channel_id=1, source_target_pairs={{0,4},{4,8},{8,12},{12,16},{16,20},{20,24},{24,28},{28,32},{32,36}... | collective-permute-start | bytes 1179656 | tf_op jit(solution)/shard_map/ppermute | solution.py:15
  383.0 249.6 %collective-permute-start.24 = (bf16[1,2,4,3,64,128]{5,3,4,1,0,2:T(4,128)(2,1)S(1)}, bf16[1,2,4,3,64,128]{5,3,4,1,0,2:T(4,128)(2,1)S(1)}, u32[]{:S(2)}, u32[]{:S(2)}) collective-permute-start(bf16[1,2,4,3,64,128]{5,3,4,1,0,2:T(4,128)(2,1)S(1)} %maximum_bitcast_fusion), channel_id=1, source_target_pairs={{4,0},{8,4},{12,8},{16,12},{20,16},{24,20},{28,24},{32,28},{36,32}... | collective-permute-start | bytes 1179656 | tf_op jit(solution)/shard_map/ppermute | solution.py:15
  385.0 251.9 %collective-permute-start.16 = (bf16[1,2,4,3,64,128]{5,3,4,1,0,2:T(4,128)(2,1)S(1)}, bf16[1,2,4,3,64,128]{5,3,4,1,0,2:T(4,128)(2,1)}, u32[]{:S(2)}, u32[]{:S(2)}) collective-permute-start(bf16[1,2,4,3,64,128]{5,3,4,1,0,2:T(4,128)(2,1)S(1)} %maximum_bitcast_fusion), channel_id=1, source_target_pairs={{0,32},{4,36},{8,40},{12,44},{16,48},{20,52},{24,56},{28,60},{32,6... | collective-permute-start | bytes 1179656 | tf_op jit(solution)/shard_map/ppermute | solution.py:15
  389.0 254.9 %collective-permute-start.17 = (bf16[1,2,4,3,64,128]{5,3,4,1,0,2:T(4,128)(2,1)S(1)}, bf16[1,2,4,3,64,128]{5,3,4,1,0,2:T(4,128)(2,1)}, u32[]{:S(2)}, u32[]{:S(2)}) collective-permute-start(bf16[1,2,4,3,64,128]{5,3,4,1,0,2:T(4,128)(2,1)S(1)} %maximum_bitcast_fusion), channel_id=1, source_target_pairs={{0,28},{4,32},{8,36},{12,40},{16,44},{20,48},{24,52},{28,56},{32,6... | collective-permute-start | bytes 1179656 | tf_op jit(solution)/shard_map/ppermute | solution.py:15
  395.0 252.5 %collective-permute-start.18 = (bf16[1,2,4,3,64,128]{5,3,4,1,0,2:T(4,128)(2,1)S(1)}, bf16[1,2,4,3,64,128]{5,3,4,1,0,2:T(4,128)(2,1)S(1)}, u32[]{:S(2)}, u32[]{:S(2)}) collective-permute-start(bf16[1,2,4,3,64,128]{5,3,4,1,0,2:T(4,128)(2,1)S(1)} %maximum_bitcast_fusion), channel_id=1, source_target_pairs={{0,24},{4,28},{8,32},{12,36},{16,40},{20,44},{24,48},{28,52},{32,5... | collective-permute-start | bytes 1179656 | tf_op jit(solution)/shard_map/ppermute | solution.py:15
  629.0 54.6 %collective-permute-start.19 = (bf16[1,2,4,3,64,128]{5,3,4,1,0,2:T(4,128)(2,1)S(1)}, bf16[1,2,4,3,64,128]{5,3,4,1,0,2:T(4,128)(2,1)S(1)}, u32[]{:S(2)}, u32[]{:S(2)}) collective-permute-start(bf16[1,2,4,3,64,128]{5,3,4,1,0,2:T(4,128)(2,1)S(1)} %maximum_bitcast_fusion), channel_id=1, source_target_pairs={{0,20},{4,24},{8,28},{12,32},{16,36},{20,40},{24,44},{28,48},{32,5... | collective-permute-start | bytes 1179656 | tf_op jit(solution)/shard_map/ppermute | solution.py:15
  632.6 52.4 %collective-permute-start.20 = (bf16[1,2,4,3,64,128]{5,3,4,1,0,2:T(4,128)(2,1)S(1)}, bf16[1,2,4,3,64,128]{5,3,4,1,0,2:T(4,128)(2,1)S(1)}, u32[]{:S(2)}, u32[]{:S(2)}) collective-permute-start(bf16[1,2,4,3,64,128]{5,3,4,1,0,2:T(4,128)(2,1)S(1)} %maximum_bitcast_fusion), channel_id=1, source_target_pairs={{0,16},{4,20},{8,24},{12,28},{16,32},{20,36},{24,40},{28,44},{32,4... | collective-permute-start | bytes 1179656 | tf_op jit(solution)/shard_map/ppermute | solution.py:15
  636.9 49.6 %collective-permute-start.21 = (bf16[1,2,4,3,64,128]{5,3,4,1,0,2:T(4,128)(2,1)S(1)}, bf16[1,2,4,3,64,128]{5,3,4,1,0,2:T(4,128)(2,1)S(1)}, u32[]{:S(2)}, u32[]{:S(2)}) collective-permute-start(bf16[1,2,4,3,64,128]{5,3,4,1,0,2:T(4,128)(2,1)S(1)} %maximum_bitcast_fusion), channel_id=1, source_target_pairs={{0,12},{4,16},{8,20},{12,24},{16,28},{20,32},{24,36},{28,40},{32,4... | collective-permute-start | bytes 1179656 | tf_op jit(solution)/shard_map/ppermute | solution.py:15
  644.0 43.9 %collective-permute-start.22 = (bf16[1,2,4,3,64,128]{5,3,4,1,0,2:T(4,128)(2,1)S(1)}, bf16[1,2,4,3,64,128]{5,3,4,1,0,2:T(4,128)(2,1)S(1)}, u32[]{:S(2)}, u32[]{:S(2)}) collective-permute-start(bf16[1,2,4,3,64,128]{5,3,4,1,0,2:T(4,128)(2,1)S(1)} %maximum_bitcast_fusion), channel_id=1, source_target_pairs={{0,8},{4,12},{8,16},{12,20},{16,24},{20,28},{24,32},{28,36},{32,40... | collective-permute-start | bytes 1179656 | tf_op jit(solution)/shard_map/ppermute | solution.py:15
  647.5 44.0 %collective-permute-start.25 = (bf16[1,2,4,3,64,128]{5,3,4,1,0,2:T(4,128)(2,1)S(1)}, bf16[1,2,4,3,64,128]{5,3,4,1,0,2:T(4,128)(2,1)S(1)}, u32[]{:S(2)}, u32[]{:S(2)}) collective-permute-start(bf16[1,2,4,3,64,128]{5,3,4,1,0,2:T(4,128)(2,1)S(1)} %maximum_bitcast_fusion), channel_id=1, source_target_pairs={{8,0},{12,4},{16,8},{20,12},{24,16},{28,20},{32,24},{36,28},{40,32... | collective-permute-start | bytes 1179656 | tf_op jit(solution)/shard_map/ppermute | solution.py:15
  683.6 28.3 %collective-permute-start.26 = (bf16[1,2,4,3,64,128]{5,3,4,1,0,2:T(4,128)(2,1)S(1)}, bf16[1,2,4,3,64,128]{5,3,4,1,0,2:T(4,128)(2,1)S(1)}, u32[]{:S(2)}, u32[]{:S(2)}) collective-permute-start(bf16[1,2,4,3,64,128]{5,3,4,1,0,2:T(4,128)(2,1)S(1)} %maximum_bitcast_fusion), channel_id=1, source_target_pairs={{12,0},{16,4},{20,8},{24,12},{28,16},{32,20},{36,24},{40,28},{44,3... | collective-permute-start | bytes 1179656 | tf_op jit(solution)/shard_map/ppermute | solution.py:15
  685.1 30.6 %collective-permute-start.27 = (bf16[1,2,4,3,64,128]{5,3,4,1,0,2:T(4,128)(2,1)S(1)}, bf16[1,2,4,3,64,128]{5,3,4,1,0,2:T(4,128)(2,1)S(1)}, u32[]{:S(2)}, u32[]{:S(2)}) collective-permute-start(bf16[1,2,4,3,64,128]{5,3,4,1,0,2:T(4,128)(2,1)S(1)} %maximum_bitcast_fusion), channel_id=1, source_target_pairs={{16,0},{20,4},{24,8},{28,12},{32,16},{36,20},{40,24},{44,28},{48,3... | collective-permute-start | bytes 1179656 | tf_op jit(solution)/shard_map/ppermute | solution.py:15
  686.5 29.3 %collective-permute-start.28 = (bf16[1,2,4,3,64,128]{5,3,4,1,0,2:T(4,128)(2,1)S(1)}, bf16[1,2,4,3,64,128]{5,3,4,1,0,2:T(4,128)(2,1)S(1)}, u32[]{:S(2)}, u32[]{:S(2)}) collective-permute-start(bf16[1,2,4,3,64,128]{5,3,4,1,0,2:T(4,128)(2,1)S(1)} %maximum_bitcast_fusion), channel_id=1, source_target_pairs={{20,0},{24,4},{28,8},{32,12},{36,16},{40,20},{44,24},{48,28},{52,3... | collective-permute-start | bytes 1179656 | tf_op jit(solution)/shard_map/ppermute | solution.py:15
  687.9 28.0 %collective-permute-start.29 = (bf16[1,2,4,3,64,128]{5,3,4,1,0,2:T(4,128)(2,1)S(1)}, bf16[1,2,4,3,64,128]{5,3,4,1,0,2:T(4,128)(2,1)S(1)}, u32[]{:S(2)}, u32[]{:S(2)}) collective-permute-start(bf16[1,2,4,3,64,128]{5,3,4,1,0,2:T(4,128)(2,1)S(1)} %maximum_bitcast_fusion), channel_id=1, source_target_pairs={{24,0},{28,4},{32,8},{36,12},{40,16},{44,20},{48,24},{52,28},{56,3... | collective-permute-start | bytes 1179656 | tf_op jit(solution)/shard_map/ppermute | solution.py:15
  691.6 47.0 %collective-permute-start.30 = (bf16[1,2,4,3,64,128]{5,3,4,1,0,2:T(4,128)(2,1)S(1)}, bf16[1,2,4,3,64,128]{5,3,4,1,0,2:T(4,128)(2,1)S(1)}, u32[]{:S(2)}, u32[]{:S(2)}) collective-permute-start(bf16[1,2,4,3,64,128]{5,3,4,1,0,2:T(4,128)(2,1)S(1)} %maximum_bitcast_fusion), channel_id=1, source_target_pairs={{28,0},{32,4},{36,8},{40,12},{44,16},{48,20},{52,24},{56,28},{60,3... | collective-permute-start | bytes 1179656 | tf_op jit(solution)/shard_map/ppermute | solution.py:15
  711.9 41.4 %collective-permute-start.31 = (bf16[1,2,4,3,64,128]{5,3,4,1,0,2:T(4,128)(2,1)S(1)}, bf16[1,2,4,3,64,128]{5,3,4,1,0,2:T(4,128)(2,1)S(1)}, u32[]{:S(2)}, u32[]{:S(2)}) collective-permute-start(bf16[1,2,4,3,64,128]{5,3,4,1,0,2:T(4,128)(2,1)S(1)} %maximum_bitcast_fusion), channel_id=1, source_target_pairs={{32,0},{36,4},{40,8},{44,12},{48,16},{52,20},{56,24},{60,28},{64,3... | collective-permute-start | bytes 1179656 | tf_op jit(solution)/shard_map/ppermute | solution.py:15
  (131 other events, 845.1 us)
Sparse Core Ops, SparseCore 0:
  481.8 143.7 all-reduce.3
where the time goes:
time: 875 us; the launch traced here: 866 us
  waiting for transfers between devices  310 us (35%)
  other arithmetic  160 us (18%)
  loops' own time  110 us (13%)
  starting transfers between devices  82.6 us (9%)
  blocking collectives  82.6 us (9%)
  local copies, waits for them, and re-layouts  56.4 us (6%)
  matrix products  48.5 us (6%)
  between operations  15.3 us (2%)
    ppermute x32, waiting for transfers between devices, passed_along(): return lax.ppermute(value, axis, pairs)  167 us
    psum x1, waiting for transfers between devices, local(): lax.psum((grad_sums[0], grad_sums[1], grad_sums[2], grad_sums[3], grad_su...  143 us
    psum x1, blocking collectives, local(): lax.psum((grad_sums[0], grad_sums[1], grad_sums[2], grad_sums[3], grad_su...  82.6 us
    ppermute x32, starting transfers between devices, passed_along(): return lax.ppermute(value, axis, pairs)  82.5 us
    another operation x1, loops' own time, local(): lax.scan(first_step, grad_sums, jnp.arange(slot_count))  63 us
    another operation x1, loops' own time, local(): outputs = [lax.map(second_step, jnp.arange(slot_count))]  47.2 us
    reduce_sum x6, other arithmetic, kernel_terms(): line_terms.append(jnp.sum(grad_values * window, axis=(0, 1)))  47.1 us
    dynamic_update_slice x2, other arithmetic, local(): lax.scan(first_step, grad_sums, jnp.arange(slot_count))  33.4 us
  transfers between devices with their start and end apart: 33, of which 18 were waited for; matrix products, arithmetic and copies ran while one was open for 1% of the time, Pallas kernels for 0%

commit v1 on v0

--- a/solution.py
+++ b/solution.py
@@ -4,6 +4,7 @@
 import jax.numpy as jnp
 from jax import lax
 from jax.sharding import PartitionSpec as P
+from jax.lax import psum
 
 TROWS = 8
 EPSILON = 1e-06
@@ -254,19 +255,22 @@
         return (result * keep_flag).astype(jnp.bfloat16)
 
     outputs = [lax.map(second_step, jnp.arange(slot_count))]
-    summed = lax.psum(
-        (
-            grad_sums[0],
-            grad_sums[1],
-            grad_sums[2],
-            grad_sums[3],
-            grad_sums[4],
-            grad_sums[5],
-            grad_sums[6],
-            grad_sums[7],
-            grad_sums[8],
+    summed = psum(
+        psum(
+            (
+                grad_sums[0],
+                grad_sums[1],
+                grad_sums[2],
+                grad_sums[3],
+                grad_sums[4],
+                grad_sums[5],
+                grad_sums[6],
+                grad_sums[7],
+                grad_sums[8],
+            ),
+            axis_name="dp",
         ),
-        ("tile", "dp"),
+        axis_name="tile",
     )
     grad_scale = 1.0 / math.sqrt(
         samples * lax.axis_size("dp") * slot_count * tile_count * extent * extent

time: 875 us -> 782 us (0.89)
  waiting for transfers between devices: 310 us -> 178 us
  blocking collectives: 82.6 us -> 135 us
  starting transfers between devices: 82.6 us -> 72.2 us
    psum x1 -> x2, waiting for transfers between devices: 143 us -> 2.7 us  [the longest x1 2.68 us: local(): psum(psum((grad_sums[0], grad_sums[1], grad_sums[2], grad_sums[3], grad_s...]
    psum x1 -> x2, blocking collectives: 82.6 us -> 135 us  [the longest x1 120 us: local(): psum(psum((grad_sums[0], grad_sums[1], grad_sums[2], grad_sums[3], grad_s...]
    ppermute x32, starting transfers between devices: 82.5 us -> 72.1 us  [passed_along(): return lax.ppermute(value, axis, pairs)]
  transfers between devices with their start and end apart: 33 -> 34, of which waited for: 18 -> 19; matrix products, arithmetic and copies ran while one was open for 1% -> 8% of each run, Pallas kernels for 0% -> 0%
where the time goes in v1:
time: 782 us; the launch traced here: 773 us
  waiting for transfers between devices  178 us (23%)
  other arithmetic  160 us (20%)
  blocking collectives  135 us (17%)
  loops' own time  110 us (14%)
  starting transfers between devices  72.2 us (9%)
  local copies, waits for them, and re-layouts  54.1 us (7%)
  matrix products  48.5 us (6%)
  between operations  15.3 us (2%)
    ppermute x32, waiting for transfers between devices, passed_along(): return lax.ppermute(value, axis, pairs)  175 us
    psum x1, blocking collectives, local(): psum(psum((grad_sums[0], grad_sums[1], grad_sums[2], grad_sums[3], grad_s...  120 us
    ppermute x32, starting transfers between devices, passed_along(): return lax.ppermute(value, axis, pairs)  72.1 us
    another operation x1, loops' own time, local(): lax.scan(first_step, grad_sums, jnp.arange(slot_count))  63 us
    reduce_sum x6, other arithmetic, kernel_terms(): line_terms.append(jnp.sum(grad_values * window, axis=(0, 1)))  47.1 us
    another operation x1, loops' own time, local(): outputs = [lax.map(second_step, jnp.arange(slot_count))]  46.6 us
    dynamic_update_slice x2, other arithmetic, local(): lax.scan(first_step, grad_sums, jnp.arange(slot_count))  33.4 us
    reduce_sum x2, other arithmetic, layer_rows(): mean_value = jnp.mean(conv_rows, -1, keepdims=True)  32.5 us
  transfers between devices with their start and end apart: 34, of which 19 were waited for; matrix products, arithmetic and copies ran while one was open for 8% of the time, Pallas kernels for 0%

profile of v1, /device:TPU:1, one launch (start us, length us, event | category | flops | bytes accessed | tf_op | source)
XLA Modules:
  0.0 772.7 jit_solution(12727644815052351091)
XLA Ops:
  17.4 5.7 collective-permute-start.2
  25.1 5.1 collective-permute-start.4
  35.7 13.1 %collective-permute-done.2 = bf16[1,2,4,3,64,128]{5,4,3,2,1,0:T(8,128)(2,1)S(1)} collective-permute-done((bf16[1,2,4,3,64,128]{5,4,3,2,1,0:T(8,128)(2,1)S(1)}, bf16[1,2,4,3,64,128]{5,4,3,2,1,0:T(8,128)(2,1)S(1)}, u32[]{:S(2)}, u32[]{:S(2)}) %collective-permute-start.2) | collective-permute-done | bytes 393248 | tf_op jit(solution)/shard_map/ppermute | solution.py:16
  73.0 4.9 collective-permute-done.11
  77.9 10.7 %collective-permute-done.12 = bf16[1,2,4,3,64,128]{5,4,3,2,1,0:T(8,128)(2,1)S(1)} collective-permute-done((bf16[1,2,4,3,64,128]{5,4,3,2,1,0:T(8,128)(2,1)S(1)}, bf16[1,2,4,3,64,128]{5,4,3,2,1,0:T(8,128)(2,1)S(1)}, u32[]{:S(2)}, u32[]{:S(2)}) %collective-permute-start.12) | collective-permute-done | bytes 393248 | tf_op jit(solution)/shard_map/ppermute | solution.py:16
  88.6 8.4 %collective-permute-done.13 = bf16[1,2,4,3,64,128]{5,4,3,2,1,0:T(8,128)(2,1)S(1)} collective-permute-done((bf16[1,2,4,3,64,128]{5,4,3,2,1,0:T(8,128)(2,1)S(1)}, bf16[1,2,4,3,64,128]{5,4,3,2,1,0:T(8,128)(2,1)S(1)}, u32[]{:S(2)}, u32[]{:S(2)}) %collective-permute-start.13) | collective-permute-done | bytes 393248 | tf_op jit(solution)/shard_map/ppermute | solution.py:16
  97.0 22.3 %collective-permute-done.14 = bf16[1,2,4,3,64,128]{5,4,3,2,1,0:T(8,128)(2,1)S(1)} collective-permute-done((bf16[1,2,4,3,64,128]{5,4,3,2,1,0:T(8,128)(2,1)S(1)}, bf16[1,2,4,3,64,128]{5,4,3,2,1,0:T(8,128)(2,1)S(1)}, u32[]{:S(2)}, u32[]{:S(2)}) %collective-permute-start.14) | collective-permute-done | bytes 393248 | tf_op jit(solution)/shard_map/ppermute | solution.py:16
  121.0 6.8 copy.25
  130.9 242.7 %while.43 = (s32[]{:T(128)}, f32[7,7,128]{2,1,0:T(8,128)}, f32[128]{0:T(128)}, f32[128]{0:T(128)}, f32[128]{0:T(128)}, /*index=5*/f32[128,512]{1,0:T(8,128)}, f3...) while((s32[]{:T(128)}, f32[7,7,128]{2,1,0:T(8,128)}, ...), condition=%wide.region_60.61_spmd.clone, body=%wide.region_0.60_spmd.clone.sunk | while | flops 3501007360 | bytes 273028160 | solution.py:240
  177.4 16.3 %fusion.232 = (f32[64,64]{1,0:T(8,128)S(1)}, f32[64,64,128]{2,1,0:T(8,128)S(1)}) fusion(f32[128]{0:T(128)S(1)} %get-tuple-element.1745, f32[128]{0:T(128)S(1)} %get-tuple-element.1536, bf16[67,70,128]{2,1,0:T(8,128)(2,1)S(1)} %get-tuple-element.1535, f32[128]{0:T(128)S(1)} %get-tuple-element.1537, f32[128]{0:T(128)S(1)} %get-tuple-element.1538, ...), kind=kLoop, calls=%fused_computation.494.clone.1 | loop fusion | flops 87027712 | bytes 47326208 | tf_op jit(solution)/shard_map/while/body/eval_jaxpr/reduce_sum | solution.py:104
  203.7 7.3 convert_reduce_fusion.6
  214.1 9.7 %fusion.234 = (f32[128]{0:T(128)}, f32[128]{0:T(128)}, f32[128]{0:T(128)}, f32[128]{0:T(128)}, f32[128]{0:T(128)}, /*index=5*/f32[128]{0:T(128)}, f32[128]{0:T(1...) fusion(bf16[67,70,128]{2,1,0:T(8,128)(2,1)S(1)} %get-tuple-elem, ...), kind=kLoop, calls=%fused_computation.301.clone.1 | loop fusion | flops 33027840 | bytes 24192512 | tf_op jit(solution)/shard_map/while/body/eval_jaxpr/reduce_sum | solution.py:80
  237.3 8.7 %fusion.235 = (f32[128]{0:T(128)}, f32[128]{0:T(128)}, f32[128]{0:T(128)}, f32[128]{0:T(128)}, f32[128]{0:T(128)}, /*index=5*/f32[128]{0:T(128)}, f32[128]{0:T(1...) fusion(bf16[67,70,128]{2,1,0:T(8,128)(2,1)S(1)} %get-tuple-element.1535, ...), kind=kLoop, calls=%fused_computation.283.clone.1 | loop fusion | flops 28834304 | bytes 8493056 | tf_op jit(solution)/shard_map/while/body/eval_jaxpr/reduce_sum | solution.py:80
  247.5 5.2 fusion.236
  291.4 16.3 %fusion.232 = (f32[64,64]{1,0:T(8,128)S(1)}, f32[64,64,128]{2,1,0:T(8,128)S(1)}) fusion(f32[128]{0:T(128)S(1)} %get-tuple-element.1745, f32[128]{0:T(128)S(1)} %get-tuple-element.1536, bf16[67,70,128]{2,1,0:T(8,128)(2,1)S(1)} %get-tuple-element.1535, f32[128]{0:T(128)S(1)} %get-tuple-element.1537, f32[128]{0:T(128)S(1)} %get-tuple-element.1538, ...), kind=kLoop, calls=%fused_computation.494.clone.1 | loop fusion | flops 87027712 | bytes 47326208 | tf_op jit(solution)/shard_map/while/body/eval_jaxpr/reduce_sum | solution.py:104
  317.8 7.3 convert_reduce_fusion.6
  328.1 9.7 %fusion.234 = (f32[128]{0:T(128)}, f32[128]{0:T(128)}, f32[128]{0:T(128)}, f32[128]{0:T(128)}, f32[128]{0:T(128)}, /*index=5*/f32[128]{0:T(128)}, f32[128]{0:T(1...) fusion(bf16[67,70,128]{2,1,0:T(8,128)(2,1)S(1)} %get-tuple-elem, ...), kind=kLoop, calls=%fused_computation.301.clone.1 | loop fusion | flops 33027840 | bytes 24192512 | tf_op jit(solution)/shard_map/while/body/eval_jaxpr/reduce_sum | solution.py:80
  351.3 8.7 %fusion.235 = (f32[128]{0:T(128)}, f32[128]{0:T(128)}, f32[128]{0:T(128)}, f32[128]{0:T(128)}, f32[128]{0:T(128)}, /*index=5*/f32[128]{0:T(128)}, f32[128]{0:T(1...) fusion(bf16[67,70,128]{2,1,0:T(8,128)(2,1)S(1)} %get-tuple-element.1535, ...), kind=kLoop, calls=%fused_computation.283.clone.1 | loop fusion | flops 28834304 | bytes 8493056 | tf_op jit(solution)/shard_map/while/body/eval_jaxpr/reduce_sum | solution.py:80
  361.5 5.2 fusion.236
  376.5 6.5 collective-permute-start.23
  388.3 6.0 collective-permute-start.17
  395.6 14.2 %all-reduce.2 = (f32[7,7,128]{2,1,0:T(8,128)S(1)}, f32[128]{0:T(128)S(1)}, f32[128]{0:T(128)S(1)}, f32[128]{0:T(128)S(1)}, f32[512]{0:T(512)S(1)}, /*index=5*/f32[128]{0:T(128)S(1)}, f32[128]{0:T(128)S(1)}) all-reduce(f32[7,7,128]{2,1,0:T(8,128)S(1)} %copy-done.21, f32[128]{0:T(128)S(1)} %copy-done.51, ...), channel_id=1, replica_groups=mesh['tile'=32,'dp'=4] {'dp'}, use_global_device_ids=true, to_apply=%region_63.64 | all-reduce | flops 7424 | bytes 59392 | tf_op jit(solution)/shard_map/psum | solution.py:259
  409.9 120.3 %all-reduce = (f32[7,7,128]{2,1,0:T(8,128)S(1)}, f32[128]{0:T(128)S(1)}, f32[128]{0:T(128)S(1)}, f32[128]{0:T(128)S(1)}, f32[512]{0:T(512)S(1)}, /*index=5*/f32[128]{0:T(128)S(1)}, f32[128]{0:T(128)S(1)}) all-reduce(f32[7,7,128]{2,1,0:T(8,128)S(1)} %get-tuple-element.763, ...), channel_id=1, replica_groups=mesh['tile'=32,'dp'=4] {'tile'}, use_global_device_ids=true, to_apply=%region_64.65 | all-reduce | flops 7424 | bytes 59392 | tf_op jit(solution)/shard_map/psum | solution.py:258
  538.4 28.5 %collective-permute-done.19 = bf16[1,2,4,3,64,128]{5,3,4,1,0,2:T(4,128)(2,1)S(1)} collective-permute-done((bf16[1,2,4,3,64,128]{5,3,4,1,0,2:T(4,128)(2,1)S(1)}, bf16[1,2,4,3,64,128]{5,3,4,1,0,2:T(4,128)(2,1)S(1)}, u32[]{:S(2)}, u32[]{:S(2)}) %collective-permute-start.19) | collective-permute-done | bytes 393248 | tf_op jit(solution)/shard_map/ppermute | solution.py:16
  571.2 5.5 collective-permute-done.22
  583.2 7.2 collective-permute-done.26
  591.8 23.7 %collective-permute-done.27 = bf16[1,2,4,3,64,128]{5,3,4,1,0,2:T(4,128)(2,1)S(1)} collective-permute-done((bf16[1,2,4,3,64,128]{5,3,4,1,0,2:T(4,128)(2,1)S(1)}, bf16[1,2,4,3,64,128]{5,3,4,1,0,2:T(4,128)(2,1)S(1)}, u32[]{:S(2)}, u32[]{:S(2)}) %collective-permute-start.27) | collective-permute-done | bytes 393248 | tf_op jit(solution)/shard_map/ppermute | solution.py:16
  617.3 30.6 %collective-permute-done.30 = bf16[1,2,4,3,64,128]{5,3,4,1,0,2:T(4,128)(2,1)S(1)} collective-permute-done((bf16[1,2,4,3,64,128]{5,3,4,1,0,2:T(4,128)(2,1)S(1)}, bf16[1,2,4,3,64,128]{5,3,4,1,0,2:T(4,128)(2,1)S(1)}, u32[]{:S(2)}, u32[]{:S(2)}) %collective-permute-start.30) | collective-permute-done | bytes 393248 | tf_op jit(solution)/shard_map/ppermute | solution.py:16
  648.1 7.2 collective-permute-done.31
  661.3 98.2 %while.42 = (s32[]{:T(128)}, bf16[2,64,64,128]{3,2,1,0:T(8,128)(2,1)}, s32[2]{0:T(128)S(1)}, bf16[2,64,64,128]{3,2,1,0:T(8,128)(2,1)S(1)}, s32[2,8]{1,0:T(2,128)...) while((s32[]{:T(128)}, ...), condition=%wide.region_62.63_spmd.clone, body=%wide.region_61.62_spmd.clone.sunk | while | flops 102684736 | bytes 53919052 | solution.py:257
  693.7 16.7 %bitcast_dynamic-update-slice_fusion.2 = bf16[2,64,64,128]{3,2,1,0:T(8,128)(2,1)} fusion(bf16[2,64,64,128]{3,2,1,0:T(8,128)(2,1)} %get-tuple-element.1782, s32[]{:T(128)} %get-tuple-element.1781, f32[]{:T(128)} %bitcast.632, f32[128]{0:T(128)S(1)} %get-tuple-element.1399, bf16[67,70,128]{2,1,0:T(8,128)(2,1)S(1)} %get-tuple-element.1430, ...), kind=kLoop, calls=%fused_computation.21.clone.1 | loop fusion | flops 88080384 | bytes 47310340 | tf_op jit(solution)/shard_map/while/body/jit(dynamic_update_index_in_dim)/dynamic_update_slice | solution.py:240
  742.8 16.7 %bitcast_dynamic-update-slice_fusion.2 = bf16[2,64,64,128]{3,2,1,0:T(8,128)(2,1)} fusion(bf16[2,64,64,128]{3,2,1,0:T(8,128)(2,1)} %get-tuple-element.1782, s32[]{:T(128)} %get-tuple-element.1781, f32[]{:T(128)} %bitcast.632, f32[128]{0:T(128)S(1)} %get-tuple-element.1399, bf16[67,70,128]{2,1,0:T(8,128)(2,1)S(1)} %get-tuple-element.1430, ...), kind=kLoop, calls=%fused_computation.21.clone.1 | loop fusion | flops 88080384 | bytes 47310340 | tf_op jit(solution)/shard_map/while/body/jit(dynamic_update_index_in_dim)/dynamic_update_slice | solution.py:240
  (530 shorter events, 193.6 us)
Async XLA Ops:
  7.2 652.3 %all-reduce.9.cloned.1.call-start = ((), (), s32[]{:S(2)}) async-start(), calls=%async_computation.1 | async-start | bytes 1048576 | tf_op jit(solution)/shard_map/psum | solution.py:259
  9.4 20.9 %collective-permute-start = (bf16[1,2,4,3,64,128]{5,4,3,2,1,0:T(8,128)(2,1)S(1)}, bf16[1,2,4,3,64,128]{5,4,3,2,1,0:T(8,128)(2,1)S(1)}, u32[]{:S(2)}, u32[]{:S(2)}) collective-permute-start(bf16[1,2,4,3,64,128]{5,4,3,2,1,0:T(8,128)(2,1)S(1)} %maximum_bitcast_fusion.1), channel_id=1, source_target_pairs={{0,32},{4,36},{8,40},{12,44},{16,48},{20,52},{24,56},{28,60},{32,6... | collective-permute-start | bytes 1179656 | tf_op jit(solution)/shard_map/ppermute | solution.py:16
  13.4 19.5 %collective-permute-start.1 = (bf16[1,2,4,3,64,128]{5,4,3,2,1,0:T(8,128)(2,1)S(1)}, bf16[1,2,4,3,64,128]{5,4,3,2,1,0:T(8,128)(2,1)S(1)}, u32[]{:S(2)}, u32[]{:S(2)}) collective-permute-start(bf16[1,2,4,3,64,128]{5,4,3,2,1,0:T(8,128)(2,1)S(1)} %maximum_bitcast_fusion.1), channel_id=1, source_target_pairs={{0,28},{4,32},{8,36},{12,40},{16,44},{20,48},{24,52},{28,56},{32,6... | collective-permute-start | bytes 1179656 | tf_op jit(solution)/shard_map/ppermute | solution.py:16
  17.4 31.4 %collective-permute-start.2 = (bf16[1,2,4,3,64,128]{5,4,3,2,1,0:T(8,128)(2,1)S(1)}, bf16[1,2,4,3,64,128]{5,4,3,2,1,0:T(8,128)(2,1)S(1)}, u32[]{:S(2)}, u32[]{:S(2)}) collective-permute-start(bf16[1,2,4,3,64,128]{5,4,3,2,1,0:T(8,128)(2,1)S(1)} %maximum_bitcast_fusion.1), channel_id=1, source_target_pairs={{0,24},{4,28},{8,32},{12,36},{16,40},{20,44},{24,48},{28,52},{32,5... | collective-permute-start | bytes 1179656 | tf_op jit(solution)/shard_map/ppermute | solution.py:16
  23.0 30.8 %collective-permute-start.3 = (bf16[1,2,4,3,64,128]{5,4,3,2,1,0:T(8,128)(2,1)S(1)}, bf16[1,2,4,3,64,128]{5,4,3,2,1,0:T(8,128)(2,1)S(1)}, u32[]{:S(2)}, u32[]{:S(2)}) collective-permute-start(bf16[1,2,4,3,64,128]{5,4,3,2,1,0:T(8,128)(2,1)S(1)} %maximum_bitcast_fusion.1), channel_id=1, source_target_pairs={{0,20},{4,24},{8,28},{12,32},{16,36},{20,40},{24,44},{28,48},{32,5... | collective-permute-start | bytes 1179656 | tf_op jit(solution)/shard_map/ppermute | solution.py:16
  25.1 30.7 %collective-permute-start.4 = (bf16[1,2,4,3,64,128]{5,4,3,2,1,0:T(8,128)(2,1)S(1)}, bf16[1,2,4,3,64,128]{5,4,3,2,1,0:T(8,128)(2,1)S(1)}, u32[]{:S(2)}, u32[]{:S(2)}) collective-permute-start(bf16[1,2,4,3,64,128]{5,4,3,2,1,0:T(8,128)(2,1)S(1)} %maximum_bitcast_fusion.1), channel_id=1, source_target_pairs={{0,16},{4,20},{8,24},{12,28},{16,32},{20,36},{24,40},{28,44},{32,4... | collective-permute-start | bytes 1179656 | tf_op jit(solution)/shard_map/ppermute | solution.py:16
  30.3 26.8 %collective-permute-start.5 = (bf16[1,2,4,3,64,128]{5,4,3,2,1,0:T(8,128)(2,1)S(1)}, bf16[1,2,4,3,64,128]{5,4,3,2,1,0:T(8,128)(2,1)S(1)}, u32[]{:S(2)}, u32[]{:S(2)}) collective-permute-start(bf16[1,2,4,3,64,128]{5,4,3,2,1,0:T(8,128)(2,1)S(1)} %maximum_bitcast_fusion.1), channel_id=1, source_target_pairs={{0,12},{4,16},{8,20},{12,24},{16,28},{20,32},{24,36},{28,40},{32,4... | collective-permute-start | bytes 1179656 | tf_op jit(solution)/shard_map/ppermute | solution.py:16
  32.9 25.5 %collective-permute-start.6 = (bf16[1,2,4,3,64,128]{5,4,3,2,1,0:T(8,128)(2,1)S(1)}, bf16[1,2,4,3,64,128]{5,4,3,2,1,0:T(8,128)(2,1)S(1)}, u32[]{:S(2)}, u32[]{:S(2)}) collective-permute-start(bf16[1,2,4,3,64,128]{5,4,3,2,1,0:T(8,128)(2,1)S(1)} %maximum_bitcast_fusion.1), channel_id=1, source_target_pairs={{0,8},{4,12},{8,16},{12,20},{16,24},{20,28},{24,32},{28,36},{32,40... | collective-permute-start | bytes 1179656 | tf_op jit(solution)/shard_map/ppermute | solution.py:16
  53.8 11.9 %collective-permute-start.8 = (bf16[1,2,4,3,64,128]{5,4,3,2,1,0:T(8,128)(2,1)S(1)}, bf16[1,2,4,3,64,128]{5,4,3,2,1,0:T(8,128)(2,1)S(1)}, u32[]{:S(2)}, u32[]{:S(2)}) collective-permute-start(bf16[1,2,4,3,64,128]{5,4,3,2,1,0:T(8,128)(2,1)S(1)} %maximum_bitcast_fusion.1), channel_id=1, source_target_pairs={{4,0},{8,4},{12,8},{16,12},{20,16},{24,20},{28,24},{32,28},{36,32}... | collective-permute-start | bytes 1179656 | tf_op jit(solution)/shard_map/ppermute | solution.py:16
  55.8 13.0 %collective-permute-start.9 = (bf16[1,2,4,3,64,128]{5,4,3,2,1,0:T(8,128)(2,1)S(1)}, bf16[1,2,4,3,64,128]{5,4,3,2,1,0:T(8,128)(2,1)S(1)}, u32[]{:S(2)}, u32[]{:S(2)}) collective-permute-start(bf16[1,2,4,3,64,128]{5,4,3,2,1,0:T(8,128)(2,1)S(1)} %maximum_bitcast_fusion.1), channel_id=1, source_target_pairs={{8,0},{12,4},{16,8},{20,12},{24,16},{28,20},{32,24},{36,28},{40,32... | collective-permute-start | bytes 1179656 | tf_op jit(solution)/shard_map/ppermute | solution.py:16
  57.2 14.5 %collective-permute-start.10 = (bf16[1,2,4,3,64,128]{5,4,3,2,1,0:T(8,128)(2,1)S(1)}, bf16[1,2,4,3,64,128]{5,4,3,2,1,0:T(8,128)(2,1)S(1)}, u32[]{:S(2)}, u32[]{:S(2)}) collective-permute-start(bf16[1,2,4,3,64,128]{5,4,3,2,1,0:T(8,128)(2,1)S(1)} %maximum_bitcast_fusion.1), channel_id=1, source_target_pairs={{12,0},{16,4},{20,8},{24,12},{28,16},{32,20},{36,24},{40,28},{44,3... | collective-permute-start | bytes 1179656 | tf_op jit(solution)/shard_map/ppermute | solution.py:16
  58.5 19.3 %collective-permute-start.11 = (bf16[1,2,4,3,64,128]{5,4,3,2,1,0:T(8,128)(2,1)S(1)}, bf16[1,2,4,3,64,128]{5,4,3,2,1,0:T(8,128)(2,1)S(1)}, u32[]{:S(2)}, u32[]{:S(2)}) collective-permute-start(bf16[1,2,4,3,64,128]{5,4,3,2,1,0:T(8,128)(2,1)S(1)} %maximum_bitcast_fusion.1), channel_id=1, source_target_pairs={{16,0},{20,4},{24,8},{28,12},{32,16},{36,20},{40,24},{44,28},{48,3... | collective-permute-start | bytes 1179656 | tf_op jit(solution)/shard_map/ppermute | solution.py:16
  60.2 28.4 %collective-permute-start.12 = (bf16[1,2,4,3,64,128]{5,4,3,2,1,0:T(8,128)(2,1)S(1)}, bf16[1,2,4,3,64,128]{5,4,3,2,1,0:T(8,128)(2,1)S(1)}, u32[]{:S(2)}, u32[]{:S(2)}) collective-permute-start(bf16[1,2,4,3,64,128]{5,4,3,2,1,0:T(8,128)(2,1)S(1)} %maximum_bitcast_fusion.1), channel_id=1, source_target_pairs={{20,0},{24,4},{28,8},{32,12},{36,16},{40,20},{44,24},{48,28},{52,3... | collective-permute-start | bytes 1179656 | tf_op jit(solution)/shard_map/ppermute | solution.py:16
  65.7 31.3 %collective-permute-start.13 = (bf16[1,2,4,3,64,128]{5,4,3,2,1,0:T(8,128)(2,1)S(1)}, bf16[1,2,4,3,64,128]{5,4,3,2,1,0:T(8,128)(2,1)S(1)}, u32[]{:S(2)}, u32[]{:S(2)}) collective-permute-start(bf16[1,2,4,3,64,128]{5,4,3,2,1,0:T(8,128)(2,1)S(1)} %maximum_bitcast_fusion.1), channel_id=1, source_target_pairs={{24,0},{28,4},{32,8},{36,12},{40,16},{44,20},{48,24},{52,28},{56,3... | collective-permute-start | bytes 1179656 | tf_op jit(solution)/shard_map/ppermute | solution.py:16
  68.8 50.5 %collective-permute-start.14 = (bf16[1,2,4,3,64,128]{5,4,3,2,1,0:T(8,128)(2,1)S(1)}, bf16[1,2,4,3,64,128]{5,4,3,2,1,0:T(8,128)(2,1)S(1)}, u32[]{:S(2)}, u32[]{:S(2)}) collective-permute-start(bf16[1,2,4,3,64,128]{5,4,3,2,1,0:T(8,128)(2,1)S(1)} %maximum_bitcast_fusion.1), channel_id=1, source_target_pairs={{28,0},{32,4},{36,8},{40,12},{44,16},{48,20},{52,24},{56,28},{60,3... | collective-permute-start | bytes 1179656 | tf_op jit(solution)/shard_map/ppermute | solution.py:16
  71.6 49.3 %collective-permute-start.15 = (bf16[1,2,4,3,64,128]{5,4,3,2,1,0:T(8,128)(2,1)S(1)}, bf16[1,2,4,3,64,128]{5,4,3,2,1,0:T(8,128)(2,1)S(1)}, u32[]{:S(2)}, u32[]{:S(2)}) collective-permute-start(bf16[1,2,4,3,64,128]{5,4,3,2,1,0:T(8,128)(2,1)S(1)} %maximum_bitcast_fusion.1), channel_id=1, source_target_pairs={{32,0},{36,4},{40,8},{44,12},{48,16},{52,20},{56,24},{60,28},{64,3... | collective-permute-start | bytes 1179656 | tf_op jit(solution)/shard_map/ppermute | solution.py:16
  376.5 201.6 %collective-permute-start.23 = (bf16[1,2,4,3,64,128]{5,3,4,1,0,2:T(4,128)(2,1)S(1)}, bf16[1,2,4,3,64,128]{5,3,4,1,0,2:T(4,128)(2,1)S(1)}, u32[]{:S(2)}, u32[]{:S(2)}) collective-permute-start(bf16[1,2,4,3,64,128]{5,3,4,1,0,2:T(4,128)(2,1)S(1)} %maximum_bitcast_fusion), channel_id=1, source_target_pairs={{0,4},{4,8},{8,12},{12,16},{16,20},{20,24},{24,28},{28,32},{32,36}... | collective-permute-start | bytes 1179656 | tf_op jit(solution)/shard_map/ppermute | solution.py:16
  383.0 196.6 %collective-permute-start.24 = (bf16[1,2,4,3,64,128]{5,3,4,1,0,2:T(4,128)(2,1)S(1)}, bf16[1,2,4,3,64,128]{5,3,4,1,0,2:T(4,128)(2,1)S(1)}, u32[]{:S(2)}, u32[]{:S(2)}) collective-permute-start(bf16[1,2,4,3,64,128]{5,3,4,1,0,2:T(4,128)(2,1)S(1)} %maximum_bitcast_fusion), channel_id=1, source_target_pairs={{4,0},{8,4},{12,8},{16,12},{20,16},{24,20},{28,24},{32,28},{36,32}... | collective-permute-start | bytes 1179656 | tf_op jit(solution)/shard_map/ppermute | solution.py:16
  385.0 149.1 %collective-permute-start.16 = (bf16[1,2,4,3,64,128]{5,3,4,1,0,2:T(4,128)(2,1)S(1)}, bf16[1,2,4,3,64,128]{5,3,4,1,0,2:T(4,128)(2,1)S(1)}, u32[]{:S(2)}, u32[]{:S(2)}) collective-permute-start(bf16[1,2,4,3,64,128]{5,3,4,1,0,2:T(4,128)(2,1)S(1)} %maximum_bitcast_fusion), channel_id=1, source_target_pairs={{0,32},{4,36},{8,40},{12,44},{16,48},{20,52},{24,56},{28,60},{32,6... | collective-permute-start | bytes 1179656 | tf_op jit(solution)/shard_map/ppermute | solution.py:16
  388.3 147.2 %collective-permute-start.17 = (bf16[1,2,4,3,64,128]{5,3,4,1,0,2:T(4,128)(2,1)S(1)}, bf16[1,2,4,3,64,128]{5,3,4,1,0,2:T(4,128)(2,1)S(1)}, u32[]{:S(2)}, u32[]{:S(2)}) collective-permute-start(bf16[1,2,4,3,64,128]{5,3,4,1,0,2:T(4,128)(2,1)S(1)} %maximum_bitcast_fusion), channel_id=1, source_target_pairs={{0,28},{4,32},{8,36},{12,40},{16,44},{20,48},{24,52},{28,56},{32,6... | collective-permute-start | bytes 1179656 | tf_op jit(solution)/shard_map/ppermute | solution.py:16
  394.2 142.7 %collective-permute-start.18 = (bf16[1,2,4,3,64,128]{5,3,4,1,0,2:T(4,128)(2,1)S(1)}, bf16[1,2,4,3,64,128]{5,3,4,1,0,2:T(4,128)(2,1)S(1)}, u32[]{:S(2)}, u32[]{:S(2)}) collective-permute-start(bf16[1,2,4,3,64,128]{5,3,4,1,0,2:T(4,128)(2,1)S(1)} %maximum_bitcast_fusion), channel_id=1, source_target_pairs={{0,24},{4,28},{8,32},{12,36},{16,40},{20,44},{24,48},{28,52},{32,5... | collective-permute-start | bytes 1179656 | tf_op jit(solution)/shard_map/ppermute | solution.py:16
  533.0 229.2 %all-reduce.7.cloned.1.call-start = ((), (), s32[]{:S(2)}) async-start(), calls=%async_computation | async-start | bytes 1048576 | tf_op jit(solution)/shard_map/psum | solution.py:258
  534.1 32.8 %collective-permute-start.19 = (bf16[1,2,4,3,64,128]{5,3,4,1,0,2:T(4,128)(2,1)S(1)}, bf16[1,2,4,3,64,128]{5,3,4,1,0,2:T(4,128)(2,1)S(1)}, u32[]{:S(2)}, u32[]{:S(2)}) collective-permute-start(bf16[1,2,4,3,64,128]{5,3,4,1,0,2:T(4,128)(2,1)S(1)} %maximum_bitcast_fusion), channel_id=1, source_target_pairs={{0,20},{4,24},{8,28},{12,32},{16,36},{20,40},{24,44},{28,48},{32,5... | collective-permute-start | bytes 1179656 | tf_op jit(solution)/shard_map/ppermute | solution.py:16
  535.5 32.8 %collective-permute-start.20 = (bf16[1,2,4,3,64,128]{5,3,4,1,0,2:T(4,128)(2,1)S(1)}, bf16[1,2,4,3,64,128]{5,3,4,1,0,2:T(4,128)(2,1)S(1)}, u32[]{:S(2)}, u32[]{:S(2)}) collective-permute-start(bf16[1,2,4,3,64,128]{5,3,4,1,0,2:T(4,128)(2,1)S(1)} %maximum_bitcast_fusion), channel_id=1, source_target_pairs={{0,16},{4,20},{8,24},{12,28},{16,32},{20,36},{24,40},{28,44},{32,4... | collective-permute-start | bytes 1179656 | tf_op jit(solution)/shard_map/ppermute | solution.py:16
  537.0 32.8 %collective-permute-start.21 = (bf16[1,2,4,3,64,128]{5,3,4,1,0,2:T(4,128)(2,1)S(1)}, bf16[1,2,4,3,64,128]{5,3,4,1,0,2:T(4,128)(2,1)S(1)}, u32[]{:S(2)}, u32[]{:S(2)}) collective-permute-start(bf16[1,2,4,3,64,128]{5,3,4,1,0,2:T(4,128)(2,1)S(1)} %maximum_bitcast_fusion), channel_id=1, source_target_pairs={{0,12},{4,16},{8,20},{12,24},{16,28},{20,32},{24,36},{28,40},{32,4... | collective-permute-start | bytes 1179656 | tf_op jit(solution)/shard_map/ppermute | solution.py:16
  568.3 13.5 %collective-permute-start.25 = (bf16[1,2,4,3,64,128]{5,3,4,1,0,2:T(4,128)(2,1)S(1)}, bf16[1,2,4,3,64,128]{5,3,4,1,0,2:T(4,128)(2,1)S(1)}, u32[]{:S(2)}, u32[]{:S(2)}) collective-permute-start(bf16[1,2,4,3,64,128]{5,3,4,1,0,2:T(4,128)(2,1)S(1)} %maximum_bitcast_fusion), channel_id=1, source_target_pairs={{8,0},{12,4},{16,8},{20,12},{24,16},{28,20},{32,24},{36,28},{40,32... | collective-permute-start | bytes 1179656 | tf_op jit(solution)/shard_map/ppermute | solution.py:16
  569.8 20.7 %collective-permute-start.26 = (bf16[1,2,4,3,64,128]{5,3,4,1,0,2:T(4,128)(2,1)S(1)}, bf16[1,2,4,3,64,128]{5,3,4,1,0,2:T(4,128)(2,1)S(1)}, u32[]{:S(2)}, u32[]{:S(2)}) collective-permute-start(bf16[1,2,4,3,64,128]{5,3,4,1,0,2:T(4,128)(2,1)S(1)} %maximum_bitcast_fusion), channel_id=1, source_target_pairs={{12,0},{16,4},{20,8},{24,12},{28,16},{32,20},{36,24},{40,28},{44,3... | collective-permute-start | bytes 1179656 | tf_op jit(solution)/shard_map/ppermute | solution.py:16
  576.7 38.8 %collective-permute-start.27 = (bf16[1,2,4,3,64,128]{5,3,4,1,0,2:T(4,128)(2,1)S(1)}, bf16[1,2,4,3,64,128]{5,3,4,1,0,2:T(4,128)(2,1)S(1)}, u32[]{:S(2)}, u32[]{:S(2)}) collective-permute-start(bf16[1,2,4,3,64,128]{5,3,4,1,0,2:T(4,128)(2,1)S(1)} %maximum_bitcast_fusion), channel_id=1, source_target_pairs={{16,0},{20,4},{24,8},{28,12},{32,16},{36,20},{40,24},{44,28},{48,3... | collective-permute-start | bytes 1179656 | tf_op jit(solution)/shard_map/ppermute | solution.py:16
  578.1 37.5 %collective-permute-start.28 = (bf16[1,2,4,3,64,128]{5,3,4,1,0,2:T(4,128)(2,1)S(1)}, bf16[1,2,4,3,64,128]{5,3,4,1,0,2:T(4,128)(2,1)S(1)}, u32[]{:S(2)}, u32[]{:S(2)}) collective-permute-start(bf16[1,2,4,3,64,128]{5,3,4,1,0,2:T(4,128)(2,1)S(1)} %maximum_bitcast_fusion), channel_id=1, source_target_pairs={{20,0},{24,4},{28,8},{32,12},{36,16},{40,20},{44,24},{48,28},{52,3... | collective-permute-start | bytes 1179656 | tf_op jit(solution)/shard_map/ppermute | solution.py:16
  579.6 36.1 %collective-permute-start.29 = (bf16[1,2,4,3,64,128]{5,3,4,1,0,2:T(4,128)(2,1)S(1)}, bf16[1,2,4,3,64,128]{5,3,4,1,0,2:T(4,128)(2,1)S(1)}, u32[]{:S(2)}, u32[]{:S(2)}) collective-permute-start(bf16[1,2,4,3,64,128]{5,3,4,1,0,2:T(4,128)(2,1)S(1)} %maximum_bitcast_fusion), channel_id=1, source_target_pairs={{24,0},{28,4},{32,8},{36,12},{40,16},{44,20},{48,24},{52,28},{56,3... | collective-permute-start | bytes 1179656 | tf_op jit(solution)/shard_map/ppermute | solution.py:16
  581.8 66.2 %collective-permute-start.30 = (bf16[1,2,4,3,64,128]{5,3,4,1,0,2:T(4,128)(2,1)S(1)}, bf16[1,2,4,3,64,128]{5,3,4,1,0,2:T(4,128)(2,1)S(1)}, u32[]{:S(2)}, u32[]{:S(2)}) collective-permute-start(bf16[1,2,4,3,64,128]{5,3,4,1,0,2:T(4,128)(2,1)S(1)} %maximum_bitcast_fusion), channel_id=1, source_target_pairs={{28,0},{32,4},{36,8},{40,12},{44,16},{48,20},{52,24},{56,28},{60,3... | collective-permute-start | bytes 1179656 | tf_op jit(solution)/shard_map/ppermute | solution.py:16
  590.4 64.8 %collective-permute-start.31 = (bf16[1,2,4,3,64,128]{5,3,4,1,0,2:T(4,128)(2,1)S(1)}, bf16[1,2,4,3,64,128]{5,3,4,1,0,2:T(4,128)(2,1)S(1)}, u32[]{:S(2)}, u32[]{:S(2)}) collective-permute-start(bf16[1,2,4,3,64,128]{5,3,4,1,0,2:T(4,128)(2,1)S(1)} %maximum_bitcast_fusion), channel_id=1, source_target_pairs={{32,0},{36,4},{40,8},{44,12},{48,16},{52,20},{56,24},{60,28},{64,3... | collective-permute-start | bytes 1179656 | tf_op jit(solution)/shard_map/ppermute | solution.py:16
  (132 other events, 845.7 us)
Sparse Core Ops, SparseCore 0:
  533.1 40.6 all-reduce.8
  659.6 102.5 all-reduce.6
